TPU v7x, 256 devices: a whole 4x4x8 slice. The times are simulated.
256 devices in a mesh: pipe: 8 (over y, core), expert: 32 (over z, x).
Axes of the slice: x: 4, y: 4, z: 8, core: 2. Of those that a mesh axis runs over, the one named last changes fastest.
Arguments:
- layer_input: bfloat16 [8, 2048, 2880], P('pipe', 'expert'), may hold values from -6 to 6
- grad_output: bfloat16 [8, 2048, 2880], P('pipe', 'expert'), may hold values from -6 to 6
- expert_ids: int32 [8, 2048, 4], P('pipe', 'expert'), may hold values from 0 to 127, as said below
- gate_probs: float32 [8, 2048, 4], P('pipe', 'expert'), may hold values from 0.05 to 1
- w_gate: bfloat16 [8, 11520, 2880], P('pipe', 'expert'), may hold values from -0.109375 to 0.109375
- w_up: bfloat16 [8, 11520, 2880], P('pipe', 'expert'), may hold values from -0.109375 to 0.109375
- w_down: bfloat16 [8, 11520, 2880], P('pipe', 'expert'), may hold values from -0.109375 to 0.109375
Outputs:
- grad_gate: bfloat16 [8, 11520, 2880], P('pipe', 'expert')
- grad_up: bfloat16 [8, 11520, 2880], P('pipe', 'expert')
- grad_down: bfloat16 [8, 11520, 2880], P('pipe', 'expert')
- grad_prev: bfloat16 [8, 2048, 2880], P('pipe', 'expert')
Inputs may be any that keep to these rules, and one draw needn't show every extreme that they name: `expert_ids`: in each section, within the 64 tokens of one device, no expert is named by more than 4 tokens; in each section one expert below 4, the same for all devices of that section, is named by exactly 4 tokens of every device; a token names 4 different experts.
All inputs are finite; a program needn't handle non-finite values.
Results may differ from a plain program's by a relative error of at most 0.0085.
Values may be sent and summed in bfloat16 or wider, within the bound.
A program may use at most 64 MiB of HBM per device.

v0:
```python
import jax
import jax.numpy as jnp
from jax import lax
from jax.sharding import PartitionSpec as P

SLICES = 8
CAP = 4


def from_behind(value, axis, steps):
    count = lax.axis_size(axis)
    leading, last = (max(0, -steps), min(count, count - steps))
    return lax.ppermute(value, axis, [(source, source + steps) for source in range(leading, last)])


def silu_parts(pre_gate):
    sigma = jax.nn.sigmoid(pre_gate)
    return (pre_gate * sigma, sigma * (1.0 + pre_gate * (1.0 - sigma)))


def contract_first(left, right):
    return lax.dot_general(
        left, right, (((0,), (0,)), ((), ())), preferred_element_type=jnp.float32
    )


def contract_last(left, right):
    return lax.dot_general(
        left, right, (((1,), (1,)), ((), ())), preferred_element_type=jnp.float32
    )


def expert_math(received_input, received_cotan, weight_gate, weight_up, weight_down):
    senders, slot_count, width = received_input.shape
    flat_input = received_input.reshape(senders * slot_count, width)
    flat_cotan = received_cotan.reshape(senders * slot_count, width)
    pre_gate = contract_last(flat_input, weight_gate)
    pre_up = contract_last(flat_input, weight_up)
    silu_val, silu_grad = silu_parts(pre_gate)
    hidden = (silu_val * pre_up).astype(jnp.bfloat16)
    hidden_grad = contract_last(flat_cotan, weight_down)
    grad_pre_gate = (hidden_grad * pre_up * silu_grad).astype(jnp.bfloat16)
    grad_pre_up = (hidden_grad * silu_val).astype(jnp.bfloat16)
    partial_value = jnp.dot(grad_pre_gate, weight_gate, preferred_element_type=jnp.float32)
    partial_value = partial_value + jnp.dot(
        grad_pre_up, weight_up, preferred_element_type=jnp.float32
    )
    partial_value = partial_value.astype(jnp.bfloat16).reshape(senders, slot_count, width)
    hidden_width = hidden.shape[1]
    return (
        partial_value,
        hidden.reshape(senders, slot_count, hidden_width),
        grad_pre_gate.reshape(senders, slot_count, hidden_width),
        grad_pre_up.reshape(senders, slot_count, hidden_width),
    )


def body(layer_input, grad_output, expert_ids, gate_probs, w_gate, w_up, w_down):
    inputs = layer_input[0]
    cotan = grad_output[0]
    chosen = expert_ids[0]
    probs = gate_probs[0]
    weight_gate = w_gate[0]
    weight_up = w_up[0]
    weight_down = w_down[0]
    peers = lax.axis_size("expert")
    flight = peers // SLICES
    token_count, top_count = chosen.shape
    width = inputs.shape[1]
    capacity = CAP
    flat_ids = chosen.reshape(token_count * top_count)
    labels = jnp.arange(flight, dtype=jnp.int32)
    matched = (flat_ids[:, None] == labels[None, :]).astype(jnp.int32)
    ranks = jnp.cumsum(matched, axis=0) - 1
    slot_ids = jnp.arange(capacity, dtype=jnp.int32)
    chooser = (matched[:, :, None] > 0) & (ranks[:, :, None] == slot_ids[None, None, :])
    chooser = chooser.reshape(token_count * top_count, flight * capacity).T.astype(jnp.bfloat16)
    token_chooser = jnp.sum(chooser.reshape(flight * capacity, token_count, top_count), axis=2)
    scaled = (probs[:, :, None] * cotan[:, None, :].astype(jnp.float32)).astype(jnp.bfloat16)
    scaled = scaled.reshape(token_count * top_count, width)
    send_input = jnp.dot(token_chooser, inputs, preferred_element_type=jnp.float32).astype(
        jnp.bfloat16
    )
    send_cotan = jnp.dot(chooser, scaled, preferred_element_type=jnp.float32).astype(jnp.bfloat16)
    send_input = jnp.repeat(send_input.reshape(flight, capacity, width), SLICES, axis=0)
    send_cotan = jnp.repeat(send_cotan.reshape(flight, capacity, width), SLICES, axis=0)
    received_input, received_cotan = (
        lax.all_to_all(send_input, "expert", split_axis=0, concat_axis=0, tiled=True),
        lax.all_to_all(send_cotan, "expert", split_axis=0, concat_axis=0, tiled=True),
    )
    partial_value, hidden, grad_pre_gate, grad_pre_up = expert_math(
        received_input, received_cotan, weight_gate, weight_up, weight_down
    )
    returned = lax.all_to_all(partial_value, "expert", split_axis=0, concat_axis=0, tiled=True)
    slot_total = received_input.shape[0] * received_input.shape[1]
    flat_input = received_input.reshape(slot_total, width)
    flat_cotan = received_cotan.reshape(slot_total, width)
    hidden_width = hidden.shape[2]
    grad_down = contract_first(hidden.reshape(slot_total, hidden_width), flat_cotan).astype(
        jnp.bfloat16
    )
    grad_gate = contract_first(grad_pre_gate.reshape(slot_total, hidden_width), flat_input).astype(
        jnp.bfloat16
    )
    grad_up = contract_first(grad_pre_up.reshape(slot_total, hidden_width), flat_input).astype(
        jnp.bfloat16
    )
    combined = jnp.sum(
        returned.astype(jnp.float32).reshape(flight, SLICES, capacity, width), axis=1
    )
    combined = combined.reshape(flight * capacity, width)
    input_grad = jnp.dot(
        token_chooser.T.astype(jnp.float32),
        combined,
        precision=lax.Precision.HIGHEST,
        preferred_element_type=jnp.float32,
    )
    shifted = from_behind(input_grad.astype(jnp.bfloat16)[None], "pipe", -1)
    return (grad_gate[None], grad_up[None], grad_down[None], shifted)


def solution(mesh):
    return jax.shard_map(
        body,
        mesh=mesh,
        in_specs=(
            P("pipe", "expert", None),
            P("pipe", "expert", None),
            P("pipe", "expert", None),
            P("pipe", "expert", None),
            P("pipe", "expert", None),
            P("pipe", "expert", None),
            P("pipe", "expert", None),
        ),
        out_specs=(
            P("pipe", "expert", None),
            P("pipe", "expert", None),
            P("pipe", "expert", None),
            P("pipe", "expert", None),
        ),
        check_vma=False,
    )
```

profile of v0, /device:TPU:1, one launch (start us, length us, event | category | flops | bytes accessed | tf_op | source)
XLA Modules:
  0.0 118.3 jit_solution(8107976542198874943)
XLA Ops:
  0.6 0.0 copy-start
  0.7 0.9 copy.28
  1.6 0.1 eq.64
  1.7 0.1 eq.60
  1.8 0.1 eq.73
  1.9 1.2 %reduce-window.6 = s32[4,2,128]{2,1,0:T(2,128)S(1)} reduce-window(s32[4,2,128]{2,1,0:T(2,128)S(1)} %compare_convert_fusion, s32[]{:T(128)} %constant.4.clone.1), window={size=1x1x128 pad=0_0x0_0x127_0}, to_apply=%region_0.0 | reduce-window | flops 130048 | bytes 8196 | tf_op jit(solution)/shard_map/reduce-window
  3.1 0.1 slice.8
  3.2 0.1 copy.30
  3.4 0.1 copy.31
  3.5 0.1 add_bitcast_fusion
  3.6 0.1 fusion.18
  3.7 0.1 copy.33
  3.8 0.1 reduce_sum.21
  3.9 1.2 %convolution_convert_fusion.5 = bf16[16,2880]{1,0:T(8,128)(2,1)S(1)} fusion(bf16[16,64]{0,1:T(8,128)(2,1)S(1)} %reduce_sum.21, bf16[1,64,2880]{2,1,0:T(8,128)(2,1)} %param.7), kind=kOutput, calls=%fused_computation.11 | convolution fusion | flops 5944320 | bytes 462848 | tf_op jit(solution)/shard_map/dot_general | solution.py:81
  5.1 1.1 broadcast_in_dim.23
  6.2 11.9 %all-to-all-start.1 = ((bf16[32,4,2880]{2,1,0:T(4,128)(2,1)}), bf16[32,4,2880]{2,1,0:T(4,128)(2,1)S(1)}, u32[]{:S(2)}, u32[]{:S(2)}) async-start(bf16[32,4,2880]{2,1,0:T(4,128)(2,1)} %bitcast.68), calls=%async_computation.1 | async-start | bytes 1507328 | tf_op jit(solution)/shard_map/all_to_all | solution.py:88
  18.1 0.1 copy.32
  18.2 0.1 bitcast_convert_fusion
  18.3 1.7 %multiply_convert_fusion = bf16[64,4,2880]{2,1,0:T(4,128)(2,1)} fusion(f32[64,2880]{1,0:T(8,128)S(1)} %bitcast_convert_fusion, f32[64,4]{1,0:T(8,128)S(1)} %copy.32), kind=kLoop, calls=%fused_computation.12 | loop fusion | flops 1474560 | bytes 2212864 | tf_op jit(solution)/shard_map/convert_element_type | solution.py:79
  20.0 3.6 %convert_element_type.78 = bf16[256,2880]{1,0:T(8,128)(2,1)} reshape(bf16[64,4,2880]{2,1,0:T(4,128)(2,1)} %multiply_convert_fusion) | data formatting | bytes 2949120 | tf_op jit(solution)/shard_map/convert_element_type | solution.py:79
  23.6 1.7 %convolution_convert_fusion.4 = bf16[16,2880]{1,0:T(8,128)(2,1)S(1)} fusion(pred[256,16]{0,1:T(8,128)(4,1)S(1)} %and.24, bf16[256,2880]{1,0:T(8,128)(2,1)} %convert_element_type.78), kind=kOutput, calls=%fused_computation.10 | convolution fusion | flops 23639040 | bytes 1570816 | tf_op jit(solution)/shard_map/dot_general | solution.py:84
  25.3 13.3 %all-to-all-done.1 = bf16[32,4,2880]{2,1,0:T(4,128)(2,1)S(1)} async-done(((bf16[32,4,2880]{2,1,0:T(4,128)(2,1)}), bf16[32,4,2880]{2,1,0:T(4,128)(2,1)S(1)}, u32[]{:S(2)}, u32[]{:S(2)}) %all-to-all-start.1) | async-done | bytes 737312 | tf_op jit(solution)/shard_map/all_to_all | solution.py:88
  38.6 1.1 broadcast_in_dim.22
  39.7 5.8 %all-to-all-start = ((bf16[32,4,2880]{2,1,0:T(4,128)(2,1)}), bf16[32,4,2880]{2,1,0:T(4,128)(2,1)}, u32[]{:S(2)}, u32[]{:S(2)}) async-start(bf16[32,4,2880]{2,1,0:T(4,128)(2,1)} %bitcast.69), calls=%async_computation | async-start | bytes 1507328 | tf_op jit(solution)/shard_map/all_to_all | solution.py:89
  45.5 1.6 %reshape.184 = bf16[128,2880]{1,0:T(8,128)(2,1)S(1)} reshape(bf16[32,4,2880]{2,1,0:T(4,128)(2,1)} %copy-done.3) | data formatting | bytes 1474560 | tf_op jit(solution)/shard_map/reshape | solution.py:35
  47.1 0.0 copy-start.1
  47.1 0.7 fusion.7
  47.8 0.8 copy-done.1
  48.7 0.7 fusion.10
  49.4 0.0 copy-start.5
  49.4 15.2 %all-to-all-done = bf16[32,4,2880]{2,1,0:T(4,128)(2,1)} async-done(((bf16[32,4,2880]{2,1,0:T(4,128)(2,1)}), bf16[32,4,2880]{2,1,0:T(4,128)(2,1)}, u32[]{:S(2)}, u32[]{:S(2)}) %all-to-all-start) | async-done | bytes 737312 | tf_op jit(solution)/shard_map/all_to_all | solution.py:89
  64.6 2.3 %reshape.179 = bf16[128,2880]{1,0:T(8,128)(2,1)} reshape(bf16[32,4,2880]{2,1,0:T(4,128)(2,1)} %all-to-all-done) | data formatting | bytes 1474560 | tf_op jit(solution)/shard_map/reshape | solution.py:36
  66.9 2.6 %multiply_convert_fusion.2 = (bf16[128,360]{0,1:T(8,128)(2,1)S(1)}, bf16[128,360]{0,1:T(8,128)(2,1)S(1)}) fusion(f32[128,360]{0,1:T(8,128)S(1)} %fusion.7, f32[128,360]{0,1:T(8,128)S(1)} %fusion.10, bf16[128,2880]{1,0:T(8,128)(2,1)} %reshape.179, bf16[1,360,2880]{2,1,0:T(8,128)(2,1)} %param.13), kind=kOutput, calls=%fused_computation.26 | convolution fusion | flops 266019840 | bytes 3363840 | tf_op jit(solution)/shard_map/dot_general | solution.py:28
  69.5 0.0 copy-start.2
  69.5 1.0 fusion.5
  70.5 0.6 copy-done.2
  71.1 1.9 %fusion.3 = bf16[128,2880]{0,1:T(8,128)(2,1)} fusion(f32[128,2880]{0,1:T(8,128)S(1)} %fusion.5, bf16[128,360]{0,1:T(8,128)(2,1)S(1)} %get-tuple-element.4, bf16[1,360,2880]{2,1,0:T(8,128)(2,1)S(1)} %copy-done.2), kind=kOutput, calls=%fused_computation.7 | convolution fusion | flops 266158080 | bytes 4377600 | tf_op jit(solution)/shard_map/dot_general | solution.py:45
  73.0 2.3 %copy.34 = bf16[128,2880]{1,0:T(8,128)(2,1)} copy(bf16[128,2880]{0,1:T(8,128)(2,1)} %fusion.3) | data formatting | bytes 1474560 | tf_op jit(solution)/shard_map/convert_element_type | solution.py:48
  75.3 2.3 %reshape.185 = bf16[32,4,2880]{2,1,0:T(4,128)(2,1)} reshape(bf16[128,2880]{1,0:T(8,128)(2,1)} %copy.34) | data formatting | bytes 1474560 | tf_op jit(solution)/shard_map/reshape | solution.py:48
  77.6 25.8 %all_to_all.15 = bf16[32,4,2880]{2,1,0:T(4,128)(2,1)S(1)} all-to-all(bf16[32,4,2880]{2,1,0:T(4,128)(2,1)} %reshape.185), channel_id=1, replica_groups=mesh['pipe'=8,'expert'=32] {'expert'}, dimensions={0} | all-to-all | bytes 1474560 | tf_op jit(solution)/shard_map/all_to_all | solution.py:94
  103.4 0.3 convert_reduce_fusion
  103.7 0.1 reshape.188
  103.8 0.4 fusion.4
  104.3 6.2 %collective-permute-start = (bf16[1,64,2880]{2,1,0:T(8,128)(2,1)S(1)}, bf16[1,64,2880]{2,1,0:T(8,128)(2,1)S(1)}, u32[]{:S(2)}, u32[]{:S(2)}) collective-permute-start(bf16[1,64,2880]{2,1,0:T(8,128)(2,1)S(1)} %fusion.4), channel_id=1, source_target_pairs={{32,0},{64,32},{96,64},{128,96},{160,128},{192,160},{224,192},{33,... | collective-permute-start | bytes 1105928 | tf_op jit(solution)/shard_map/ppermute | solution.py:13
  110.4 2.9 %fusion.1 = bf16[1,360,2880]{2,1,0:T(8,128)(2,1)} fusion(bf16[128,360]{0,1:T(8,128)(2,1)} %copy-done.8, bf16[128,2880]{1,0:T(8,128)(2,1)S(1)} %reshape.184), kind=kOutput, calls=%fused_computation.4 | convolution fusion | flops 266457600 | bytes 2903040 | tf_op jit(solution)/shard_map/dot_general | solution.py:22
  113.4 2.1 %fusion = bf16[1,360,2880]{2,1,0:T(8,128)(2,1)} fusion(bf16[128,360]{0,1:T(8,128)(2,1)S(1)} %get-tuple-element.5, bf16[128,2880]{1,0:T(8,128)(2,1)S(1)} %reshape.184), kind=kOutput, calls=%fused_computation.3 | convolution fusion | flops 266457600 | bytes 2903040 | tf_op jit(solution)/shard_map/dot_general | solution.py:22
  115.4 2.1 %fusion.2 = bf16[1,360,2880]{2,1,0:T(8,128)(2,1)} fusion(bf16[128,2880]{1,0:T(8,128)(2,1)S(1)} %copy-done.4, f32[128,360]{0,1:T(8,128)S(1)} %copy-done.6, f32[128,360]{0,1:T(8,128)S(1)} %fusion.7), kind=kOutput, calls=%fused_computation.5 | convolution fusion | flops 266734080 | bytes 3179520 | tf_op jit(solution)/shard_map/dot_general | solution.py:22
  117.5 0.7 copy.39
  (29 shorter events, 0.2 us)
Async XLA Ops:
  0.6 46.4 %copy-start = (bf16[1,360,2880]{2,1,0:T(8,128)(2,1)S(1)}, bf16[1,360,2880]{2,1,0:T(8,128)(2,1)}, u32[]{:S(2)}) copy-start(bf16[1,360,2880]{2,1,0:T(8,128)(2,1)} %param.11) | copy-start | bytes 6220804
  0.6 17.5 %copy-start.9 = (f32[1,64,4]{1,2,0:T(4,128)S(1)}, f32[1,64,4]{1,2,0:T(4,128)}, u32[]{:S(2)}) copy-start(f32[1,64,4]{1,2,0:T(4,128)} %param.10) | copy-start | bytes 3076
  0.7 17.6 %copy-start.7 = (bf16[1,64,2880]{2,1,0:T(8,128)(2,1)S(1)}, bf16[1,64,2880]{2,1,0:T(8,128)(2,1)}, u32[]{:S(2)}) copy-start(bf16[1,64,2880]{2,1,0:T(8,128)(2,1)} %param.8) | copy-start | bytes 1105924
  6.2 32.4 %all-to-all-start.1 = ((bf16[32,4,2880]{2,1,0:T(4,128)(2,1)}), bf16[32,4,2880]{2,1,0:T(4,128)(2,1)S(1)}, u32[]{:S(2)}, u32[]{:S(2)}) async-start(bf16[32,4,2880]{2,1,0:T(4,128)(2,1)} %bitcast.68), calls=%async_computation.1 | async-start | bytes 1507328 | tf_op jit(solution)/shard_map/all_to_all | solution.py:88
  38.6 1.1 copy-start.3
  39.7 24.9 %all-to-all-start = ((bf16[32,4,2880]{2,1,0:T(4,128)(2,1)}), bf16[32,4,2880]{2,1,0:T(4,128)(2,1)}, u32[]{:S(2)}, u32[]{:S(2)}) async-start(bf16[32,4,2880]{2,1,0:T(4,128)(2,1)} %bitcast.69), calls=%async_computation | async-start | bytes 1507328 | tf_op jit(solution)/shard_map/all_to_all | solution.py:89
  47.1 1.6 %copy-start.1 = (bf16[1,360,2880]{2,1,0:T(8,128)(2,1)S(1)}, bf16[1,360,2880]{2,1,0:T(8,128)(2,1)}, u32[]{:S(2)}) copy-start(bf16[1,360,2880]{2,1,0:T(8,128)(2,1)} %param.12) | copy-start | bytes 6220804
  49.4 20.0 %copy-start.5 = (f32[128,360]{0,1:T(8,128)}, f32[128,360]{0,1:T(8,128)S(1)}, u32[]{:S(2)}) copy-start(f32[128,360]{0,1:T(8,128)S(1)} %fusion.10) | copy-start | bytes 552964
  69.5 3.6 %copy-start.8 = (bf16[128,360]{0,1:T(8,128)(2,1)}, bf16[128,360]{0,1:T(8,128)(2,1)S(1)}, u32[]{:S(2)}) copy-start(bf16[128,360]{0,1:T(8,128)(2,1)S(1)} %get-tuple-element.4) | copy-start | bytes 276484
  69.5 1.6 %copy-start.2 = (bf16[1,360,2880]{2,1,0:T(8,128)(2,1)S(1)}, bf16[1,360,2880]{2,1,0:T(8,128)(2,1)}, u32[]{:S(2)}) copy-start(bf16[1,360,2880]{2,1,0:T(8,128)(2,1)} %param.12) | copy-start | bytes 6220804
  104.3 13.3 %collective-permute-start = (bf16[1,64,2880]{2,1,0:T(8,128)(2,1)S(1)}, bf16[1,64,2880]{2,1,0:T(8,128)(2,1)S(1)}, u32[]{:S(2)}, u32[]{:S(2)}) collective-permute-start(bf16[1,64,2880]{2,1,0:T(8,128)(2,1)S(1)} %fusion.4), channel_id=1, source_target_pairs={{32,0},{64,32},{96,64},{128,96},{160,128},{192,160},{224,192},{33,... | collective-permute-start | bytes 1105928 | tf_op jit(solution)/shard_map/ppermute | solution.py:13
  113.4 2.1 %copy-start.4 = (bf16[128,2880]{1,0:T(8,128)(2,1)S(1)}, bf16[128,2880]{1,0:T(8,128)(2,1)}, u32[]{:S(2)}) copy-start(bf16[128,2880]{1,0:T(8,128)(2,1)} %reshape.179) | copy-start | bytes 2211844
  113.4 2.1 %copy-start.6 = (f32[128,360]{0,1:T(8,128)S(1)}, f32[128,360]{0,1:T(8,128)}, u32[]{:S(2)}) copy-start(f32[128,360]{0,1:T(8,128)} %copy-done.5) | copy-start | bytes 552964
where the time goes:
time: 119 us; the launch traced here: 118 us
  waiting for transfers between devices  28.4 us (24%)
  blocking collectives  25.8 us (22%)
  starting transfers between devices  23.8 us (20%)
  local copies, waits for them, and re-layouts  18.3 us (15%)
  matrix products  17.4 us (15%)
  other arithmetic  3.67 us (3%)
    all_to_all x1, blocking collectives, body(): lax.all_to_all(partial_value, 'expert', split_axis=0, concat_axis=0, tile...  25.8 us
    all_to_all x1, waiting for transfers between devices, body(): lax.all_to_all(send_cotan, 'expert', split_axis=0, concat_axis=0, tiled=T...  15.2 us
    all_to_all x1, waiting for transfers between devices, body(): lax.all_to_all(send_input, 'expert', split_axis=0, concat_axis=0, tiled=T...  13.3 us
    all_to_all x1, starting transfers between devices, body(): lax.all_to_all(send_input, 'expert', split_axis=0, concat_axis=0, tiled=T...  11.9 us
    dot_general x3, matrix products, contract_first(): lax.dot_general(left, right, (((0,), (0,)), ((), ())), preferred_element_...  7.07 us
    ppermute x1, starting transfers between devices, from_behind(): lax.ppermute(value, axis, [(source, source + steps) for source in range(l...  6.17 us
    all_to_all x1, starting transfers between devices, body(): lax.all_to_all(send_cotan, 'expert', split_axis=0, concat_axis=0, tiled=T...  5.76 us
    dot_general x3, matrix products, contract_last(): lax.dot_general(left, right, (((1,), (1,)), ((), ())), preferred_element_...  4.06 us
  transfers between devices with their start and end apart: 3, of which 2 were waited for; matrix products, arithmetic and copies ran while one was open for 15% of the time, Pallas kernels for 0%

commit v1 on v0

v1 whole, which is shorter than its diff:
```python
import jax
import jax.numpy as jnp
from jax import lax
from jax.experimental import pallas as pl
from jax.experimental.pallas import tpu as pltpu
from jax.sharding import PartitionSpec as P

D = 2880
HS = 360
TOK = 64
FLIGHT = 4
NX = 4
NZ = 8
HALF = 1408
WIDE = D - HALF
CHUNKS = ((0, 768), (768, WIDE))
ARRIVAL = (0, 1, 7, 2, 6, 3, 5, 4)
LAG = 3
MESH = pl.DeviceIdType.MESH
F32 = jnp.float32
BF16 = jnp.bfloat16


def nt(left, right):
    return lax.dot_general(left, right, (((1,), (1,)), ((), ())), preferred_element_type=F32)


def nn(left, right):
    return jnp.dot(left, right, preferred_element_type=F32)


def selector(ids, rows, per_expert):
    row = lax.broadcasted_iota(jnp.int32, (rows, TOK), 0)
    owner = row // per_expert
    matches = [ids[k : k + 1, :] == owner for k in range(4)]
    hit = matches[0] | matches[1] | matches[2] | matches[3]
    before = lax.broadcasted_iota(jnp.int32, (TOK, TOK), 0)
    token = lax.broadcasted_iota(jnp.int32, (TOK, TOK), 1)
    earlier = jnp.where(before < token, 1.0, 0.0).astype(BF16)
    rank = nn(jnp.where(hit, 1.0, 0.0).astype(BF16), earlier)
    return jnp.where(hit & (rank == (row % 4).astype(F32)), 1.0, 0.0), matches, row % 8 < 4


def kernel(
    x_hbm, g_hbm, ids_hbm, pr_hbm, wg_hbm, wu_hbm, wd_hbm,
    gg_hbm, gu_hbm, gd_hbm, gp_hbm,
    x_v, g_v, ids_v, ids2_v, pr_v, wg_v, wu_v, wd_v, send_v, rows_v,
    part_v, gg_v, gu_v, gd_v, gp_v,
    q1a, q1b, q2a, q2b, ta, tb, fa, fb,
    lsem, osem, sem_z, sem_x, sem_f, sem_r, sem_ids, s1, r1, s2, r2, s3, r3,
):
    pipe = lax.axis_index("pipe")
    me = lax.axis_index("expert")
    z = lax.div(me, NX)
    x = lax.rem(me, NX)
    xr = lax.rem(x + 1, NX)
    xl = lax.rem(x + NX - 1, NX)
    xo = lax.rem(x + 2, NX)

    def same(zz, xx):
        return {"pipe": pipe, "expert": zz * NX + xx}

    loads = [
        pltpu.make_async_copy(src.at[0], dst, lsem.at[i])
        for i, (src, dst) in enumerate(
            (
                (ids_hbm, ids_v),
                (pr_hbm, pr_v),
                (x_hbm, x_v),
                (g_hbm, g_v),
                (wg_hbm, wg_v),
                (wu_hbm, wu_v),
                (wd_hbm, wd_v),
            )
        )
    ]
    for load in loads:
        load.start()

    barrier = pltpu.get_barrier_semaphore()
    for d in range(1, NZ):
        pl.semaphore_signal(barrier, 1, device_id=same(lax.rem(z + d, NZ), x), device_id_type=MESH)
    for xn in (xl, xr):
        pl.semaphore_signal(barrier, 1, device_id=same(z, xn), device_id_type=MESH)

    @pl.when(pipe > 0)
    def _():
        for d in range(NZ):
            pl.semaphore_signal(
                barrier, 1, device_id={"pipe": pipe - 1, "expert": lax.rem(z + d, NZ) * NX + x},
                device_id_type=MESH,
            )

    @pl.when(pipe < 7)
    def _():
        for d in range(NZ):
            pl.semaphore_signal(
                barrier, 1, device_id={"pipe": pipe + 1, "expert": lax.rem(z + d, NZ) * NX + x},
                device_id_type=MESH,
            )

    loads[0].wait()
    loads[1].wait()
    ids = ids_v[...]
    sel, matches, is_in = selector(ids, 32, 8)
    probs = pr_v[...]
    weight = jnp.zeros((32, TOK), F32)
    for k in range(4):
        weight = weight + jnp.where(matches[k], probs[k : k + 1, :], 0.0)
    weight_col = jnp.sum(weight * sel, axis=1, keepdims=True)
    sel_in = jnp.where(is_in, sel, 0.0).astype(BF16)
    sel_co = jnp.where(is_in, 0.0, sel).astype(BF16)
    loads[2].wait()
    loads[3].wait()
    picked = nn(sel_in, x_v[...]) + nn(sel_co, g_v[...]) * weight_col
    send_v[...] = picked.reshape(FLIGHT, 8, D).astype(BF16)

    pl.semaphore_wait(barrier, jnp.where((pipe == 0) | (pipe == 7), 17, 25))

    def block(xs, d):
        return (xs, lax.rem(z + NZ - d, NZ))

    own = pltpu.make_async_copy(send_v.at[lax.div(z, 2)], rows_v.at[x, z], sem_r.at[x, z])
    own.start()
    z_sends = []
    for d in ARRIVAL[1:]:
        zt = lax.rem(z + d, NZ)
        z_sends.append(
            pltpu.make_async_remote_copy(
                send_v.at[lax.div(zt, 2)], rows_v.at[x, z], sem_z.at[d], sem_r.at[x, z],
                device_id=same(zt, x), device_id_type=MESH,
            )
        )
        z_sends[-1].start()

    @pl.when(pipe > 0)
    def _():
        pltpu.make_async_remote_copy(
            ids_v, ids2_v, sem_ids.at[0], sem_ids.at[1],
            device_id={"pipe": pipe - 1, "expert": me}, device_id_type=MESH,
        ).start()

    def arrived(xs, d):
        b = block(xs, d)
        return pltpu.make_async_remote_copy(
            rows_v.at[b], rows_v.at[b], sem_z.at[0], sem_r.at[b],
            device_id=same(z, xr), device_id_type=MESH,
        )

    x_sends = []

    def push(xs, d, to, sem):
        b = block(xs, d)
        x_sends.append(
            pltpu.make_async_remote_copy(
                rows_v.at[b], rows_v.at[b], sem, sem_r.at[b], device_id=same(z, to), device_id_type=MESH
            )
        )
        x_sends[-1].start()

    def forward(d):
        arrived(xl, d).wait_recv()
        arrived(xr, d).wait_recv()
        if d % 2 == 0:
            push(xl, d, xr, sem_f.at[d])
        else:
            push(xr, d, xl, sem_f.at[d])

    for i, d in enumerate(ARRIVAL):
        if d == 0:
            own.wait()
        else:
            arrived(x, d).wait_recv()
        push(x, d, xr, sem_x.at[0, d])
        push(x, d, xl, sem_x.at[1, d])
        if i >= LAG:
            forward(ARRIVAL[i - LAG])
    for d in ARRIVAL[NZ - LAG :]:
        forward(d)
    for load in loads[4:]:
        load.wait()
    for d in ARRIVAL:
        arrived(xo, d).wait_recv()

    rows = rows_v[...].reshape(256, D)
    pre_gate = nt(wg_v[...], rows)
    pre_up = nt(wu_v[...], rows)
    hidden_grad = pltpu.roll(nt(wd_v[...], rows), 252, 1)
    in_col = lax.broadcasted_iota(jnp.int32, (HS, 256), 1) % 8 < 4
    sigma = jax.nn.sigmoid(pre_gate)
    silu = pre_gate * sigma
    slope = sigma * (1.0 + pre_gate * (1.0 - sigma))
    hidden = jnp.where(in_col, silu * pre_up, 0.0)
    d_gate = jnp.where(in_col, hidden_grad * pre_up * slope, 0.0)
    d_up = jnp.where(in_col, hidden_grad * silu, 0.0)
    hidden_co = pltpu.roll(hidden, 4, 1).astype(BF16)
    gate_lo = d_gate.T.astype(BF16)
    up_lo = d_up.T.astype(BF16)
    gate_hi = pltpu.roll(d_gate, 4, 1).T.astype(BF16)
    up_hi = pltpu.roll(d_up, 4, 1).T.astype(BF16)
    d_gate = d_gate.astype(BF16)
    d_up = d_up.astype(BF16)

    mate = x + 1 - 2 * lax.rem(x, 2)
    far = NX - 1 - x
    mates = ((mate, far), (far, mate))
    q1s, q2s, ts, fs = (q1a, q1b), (q2a, q2b), (ta, tb), (fa, fb)
    tail = []

    def step1(k):
        c0, c1 = CHUNKS[k]
        first, _ = mates[k]
        other = NX - 1 - first if k == 0 else first + 1 - 2 * lax.rem(first, 2)
        out = []
        for slot, dest in enumerate((first, other)):
            out.append(
                pltpu.make_async_remote_copy(
                    part_v.at[dest, :, pl.ds(c0, c1 - c0)], q1s[k].at[slot], s1.at[k, slot], r1.at[k, slot],
                    device_id=same(z, first), device_id_type=MESH,
                )
            )
        return out

    def step2(k):
        c0, c1 = CHUNKS[k]
        _, second = mates[k]
        return pltpu.make_async_remote_copy(
            part_v.at[second, :, pl.ds(c0, c1 - c0)], q2s[k], s2.at[k], r2.at[k],
            device_id=same(z, second), device_id_type=MESH,
        )

    def step3(k, d):
        zt = lax.rem(z + d, NZ)
        return pltpu.make_async_remote_copy(
            ts[k].at[zt], fs[k].at[z], s3.at[k, d], r3.at[k, z],
            device_id={"pipe": pipe - 1, "expert": zt * NX + x}, device_id_type=MESH,
        )

    def partials(k):
        c0, c1 = CHUNKS[k]
        lo1 = min(c1, HALF)
        low = nn(gate_lo, wg_v[:, c0:lo1]) + nn(up_lo, wu_v[:, c0:lo1])
        high = nn(gate_hi, wg_v[:, HALF + c0 : HALF + c1]) + nn(up_hi, wu_v[:, HALF + c0 : HALF + c1])
        part_v[:, :, c0:lo1] = (low + high[:, : lo1 - c0]).astype(BF16).reshape(NX, 64, lo1 - c0)
        if c1 > lo1:
            part_v[:, :, lo1:c1] = high[:, lo1 - c0 :].astype(BF16).reshape(NX, 64, c1 - lo1)
        for copy in step1(k):
            copy.start()

    def reduce1(k):
        c0, c1 = CHUNKS[k]
        _, second = mates[k]
        for copy in step1(k):
            copy.wait_recv()
        part_v[second, :, c0:c1] = (
            part_v[second, :, c0:c1].astype(F32) + q1s[k][1].astype(F32)
        ).astype(BF16)
        step2(k).start()

    def reduce2(k):
        c0, c1 = CHUNKS[k]
        step2(k).wait_recv()
        total = (
            part_v[x, :, c0:c1].astype(F32) + q1s[k][0].astype(F32) + q2s[k][...].astype(F32)
        )
        ts[k][...] = total.reshape(NZ, 8, c1 - c0).astype(BF16)

        @pl.when(pipe > 0)
        def _():
            for d in range(NZ):
                step3(k, d).start()

    stores = []

    def grads(left, out_v, out_hbm, sem):
        for c0 in range(0, D, 576 * 5):
            c1 = min(c0 + 576 * 5, D)
            cols = rows_v[:, :, :, c0:c1].reshape(256, c1 - c0)
            out_v[:, c0:c1] = nn(left, cols).astype(BF16)
        stores.append(pltpu.make_async_copy(out_v, out_hbm.at[0], sem))
        stores[-1].start()

    partials(0)
    partials(1)
    grads(hidden_co, gd_v, gd_hbm, osem.at[0])
    reduce1(0)
    reduce1(1)
    grads(d_gate, gg_v, gg_hbm, osem.at[1])
    reduce2(0)
    reduce2(1)
    grads(d_up, gu_v, gu_hbm, osem.at[2])

    @pl.when(pipe == 7)
    def _():
        gp_v[...] = jnp.zeros_like(gp_v)

    @pl.when(pipe < 7)
    def _():
        pltpu.make_async_remote_copy(
            ids_v, ids2_v, sem_ids.at[0], sem_ids.at[1],
            device_id={"pipe": pipe, "expert": me}, device_id_type=MESH,
        ).wait_recv()
        sel2, _, low_half = selector(ids2_v[...], 64, 16)
        sel_lo = jnp.where(low_half, sel2, 0.0).T.astype(BF16)
        sel_hi = jnp.where(low_half, 0.0, sel2).T.astype(BF16)
        for k, (c0, c1) in enumerate(CHUNKS):
            for d in range(NZ):
                zs = lax.rem(z + d, NZ)
                pltpu.make_async_remote_copy(
                    ts[k].at[0], fs[k].at[zs], s3.at[k, 0], r3.at[k, zs],
                    device_id={"pipe": pipe, "expert": me}, device_id_type=MESH,
                ).wait_recv()
            got = fs[k][...].reshape(64, c1 - c0)
            lo1 = min(c1, HALF)
            gp_v[:, c0:lo1] = nn(sel_lo, got[:, : lo1 - c0]).astype(BF16)
            gp_v[:, HALF + c0 : HALF + c1] = nn(sel_hi, got).astype(BF16)

    last = pltpu.make_async_copy(gp_v, gp_hbm.at[0], osem.at[3])
    last.start()

    for copy in z_sends + x_sends:
        copy.wait_send()
    for k in range(2):
        for copy in step1(k):
            copy.wait_send()
        step2(k).wait_send()

    @pl.when(pipe > 0)
    def _():
        pltpu.make_async_remote_copy(
            ids_v, ids2_v, sem_ids.at[0], sem_ids.at[1],
            device_id={"pipe": pipe - 1, "expert": me}, device_id_type=MESH,
        ).wait_send()
        for k in range(2):
            for d in range(NZ):
                step3(k, d).wait_send()

    for store in stores:
        store.wait()
    last.wait()


def body(layer_input, grad_output, expert_ids, gate_probs, w_gate, w_up, w_down):
    ids = jnp.transpose(expert_ids, (0, 2, 1))
    probs = jnp.transpose(gate_probs, (0, 2, 1))
    dma = pltpu.SemaphoreType.DMA
    w0, w1 = (c1 - c0 for c0, c1 in CHUNKS)
    wide = (HS, D)
    return tuple(pl.pallas_call(
        kernel,
        out_shape=[jax.ShapeDtypeStruct((1, HS, D), BF16)] * 3 + [jax.ShapeDtypeStruct((1, TOK, D), BF16)],
        in_specs=[pl.BlockSpec(memory_space=pl.ANY)] * 7,
        out_specs=[pl.BlockSpec(memory_space=pl.ANY)] * 4,
        scratch_shapes=[
            pltpu.VMEM((TOK, D), BF16),
            pltpu.VMEM((TOK, D), BF16),
            pltpu.VMEM((4, TOK), jnp.int32),
            pltpu.VMEM((4, TOK), jnp.int32),
            pltpu.VMEM((4, TOK), F32),
            pltpu.VMEM(wide, BF16),
            pltpu.VMEM(wide, BF16),
            pltpu.VMEM(wide, BF16),
            pltpu.VMEM((FLIGHT, 8, D), BF16),
            pltpu.VMEM((NX, NZ, 8, D), BF16),
            pltpu.VMEM((NX, 64, WIDE), BF16),
            pltpu.VMEM(wide, BF16),
            pltpu.VMEM(wide, BF16),
            pltpu.VMEM(wide, BF16),
            pltpu.VMEM((TOK, D), BF16),
            pltpu.VMEM((2, 64, w0), BF16),
            pltpu.VMEM((2, 64, w1), BF16),
            pltpu.VMEM((64, w0), BF16),
            pltpu.VMEM((64, w1), BF16),
            pltpu.VMEM((NZ, 8, w0), BF16),
            pltpu.VMEM((NZ, 8, w1), BF16),
            pltpu.VMEM((NZ, 8, w0), BF16),
            pltpu.VMEM((NZ, 8, w1), BF16),
            dma((7,)),
            dma((4,)),
            dma((NZ,)),
            dma((2, NZ)),
            dma((NZ,)),
            dma((NX, NZ)),
            dma((2,)),
            dma((2, 2)),
            dma((2, 2)),
            dma((2,)),
            dma((2,)),
            dma((2, NZ)),
            dma((2, NZ)),
        ],
        compiler_params=pltpu.CompilerParams(
            collective_id=0, has_side_effects=True, vmem_limit_bytes=48 * 1024 * 1024
        ),
    )(layer_input, grad_output, ids, probs, w_gate, w_up, w_down))


def solution(mesh):
    spec = P("pipe", "expert", None)
    return jax.shard_map(body, mesh=mesh, in_specs=(spec,) * 7, out_specs=(spec,) * 4, check_vma=False)
```

time: 119 us -> 62.3 us (0.52)
  Pallas kernels: 0 us -> 52.3 us
  waiting for transfers between devices: 28.4 us -> 0 us
  blocking collectives: 25.8 us -> 0 us
  starting transfers between devices: 23.8 us -> 0 us
  matrix products: 17.4 us -> 0 us
  local copies, waits for them, and re-layouts: 18.3 us -> 9.09 us
  other arithmetic: 3.67 us -> 0 us
    pallas_call x0 -> x1, Pallas kernels: none -> 52.3 us  [body(): pl.pallas_call(kernel, out_shape=[jax.ShapeDtypeStruct((1, HS, D), BF16)]...]
    all_to_all x2 -> x0, waiting for transfers between devices: 28.4 us -> none  [the longest x1 15.2 us: body(): lax.all_to_all(send_cotan, 'expert', split_axis=0, concat_axis=0, tiled=T...]
    all_to_all x1 -> x0, blocking collectives: 25.8 us -> none  [body(): lax.all_to_all(partial_value, 'expert', split_axis=0, concat_axis=0, tile...]
    all_to_all x2 -> x0, starting transfers between devices: 17.6 us -> none  [the longest x1 11.9 us: body(): lax.all_to_all(send_input, 'expert', split_axis=0, concat_axis=0, tiled=T...]
    dot_general x11 -> x0, matrix products: 17.4 us -> none  [the longest x3 7.07 us: contract_first(): lax.dot_general(left, right, (((0,), (0,)), ((), ())), preferred_element_...]
    reshape x7 -> x0, local copies, waits for them, and re-layouts: 6.44 us -> none  [the longest x1 2.35 us: expert_math(): partial_value.astype(jnp.bfloat16).reshape(senders, slot_count, width)]
    ppermute x1 -> x0, starting transfers between devices: 6.17 us -> none  [from_behind(): lax.ppermute(value, axis, [(source, source + steps) for source in range(l...]
    unnamed x23 -> x14, local copies, waits for them, and re-layouts: 3.16 us -> 9.09 us
  transfers between devices with their start and end apart: 3 -> 0, of which waited for: 2 -> 0; matrix products, arithmetic and copies ran while one was open for 15% -> 0% of each run, Pallas kernels for 0% -> 0%
where the time goes in v1:
time: 62.3 us; the launch traced here: 62.1 us
  Pallas kernels  52.3 us (84%)
  local copies, waits for them, and re-layouts  9.09 us (15%)
  between operations  0.66 us (1%)
    pallas_call x1, Pallas kernels, body(): pl.pallas_call(kernel, out_shape=[jax.ShapeDtypeStruct((1, HS, D), BF16)]...  52.3 us
    unnamed x14, local copies, waits for them, and re-layouts  9.09 us

profile of v1, /device:TPU:1, one launch (start us, length us, event | category | flops | bytes accessed | tf_op | source)
XLA Modules:
  0.0 62.1 jit_solution(6833880368068520133)
XLA Ops:
  0.6 0.0 copy-start
  0.6 1.0 %copy-done = bf16[1,64,2880]{2,1,0:T(8,128)(2,1)S(1)} copy-done((bf16[1,64,2880]{2,1,0:T(8,128)(2,1)S(1)}, bf16[1,64,2880]{2,1,0:T(8,128)(2,1)}, u32[]{:S(2)}) %copy-start) | copy-done | bytes 368664
  1.6 0.0 copy-start.1
  1.6 1.0 %copy-done.1 = bf16[1,64,2880]{2,1,0:T(8,128)(2,1)S(1)} copy-done((bf16[1,64,2880]{2,1,0:T(8,128)(2,1)S(1)}, bf16[1,64,2880]{2,1,0:T(8,128)(2,1)}, u32[]{:S(2)}) %copy-start.1) | copy-done | bytes 368664
  2.6 0.0 copy-start.2
  2.6 0.7 %copy-done.2 = s32[1,64,4]{1,2,0:T(4,128)S(1)} copy-done((s32[1,64,4]{1,2,0:T(4,128)S(1)}, s32[1,64,4]{1,2,0:T(4,128)}, u32[]{:S(2)}) %copy-start.2) | copy-done | bytes 1048
  3.3 0.0 copy-start.3
  3.3 0.7 %copy-done.3 = f32[1,64,4]{1,2,0:T(4,128)S(1)} copy-done((f32[1,64,4]{1,2,0:T(4,128)S(1)}, f32[1,64,4]{1,2,0:T(4,128)}, u32[]{:S(2)}) %copy-start.3) | copy-done | bytes 1048
  4.0 52.3 %shard_map.102 = (bf16[1,360,2880]{2,1,0:T(8,128)(2,1)S(1)}, bf16[1,360,2880]{2,1,0:T(8,128)(2,1)S(1)}, bf16[1,360,2880]{2,1,0:T(8,128)(2,1)}, bf16[1,64,2880]{2,1,0:T(8,128)(2,1)S(1)}) custom-call(bf16[1,64,2880]{2,1,0:T(8,128)(2,1)S(1)} %copy-done, bf16[1,64,2880]{2,1,0:T(8,128)(2,1)S(1)} %copy-done.1, s32[1,4,64]{2,1,0:T(4,128)S(1)} %bitcast.2, ...), custom_call_target="tpu_custom_call" | custom-call | tf_op jit(solution)/shard_map/pallas_call | solution.py:349
  56.3 1.3 %copy.15 = bf16[1,360,2880]{2,1,0:T(8,128)(2,1)} copy(bf16[1,360,2880]{2,1,0:T(8,128)(2,1)S(1)} %get-tuple-element.8) | data formatting | bytes 4147200
  57.6 0.0 copy-start.4
  57.6 1.3 %copy.16 = bf16[1,360,2880]{2,1,0:T(8,128)(2,1)} copy(bf16[1,360,2880]{2,1,0:T(8,128)(2,1)S(1)} %get-tuple-element.9) | data formatting | bytes 4147200
  59.0 1.0 %copy-done.4 = bf16[1,360,2880]{2,1,0:T(8,128)(2,1)S(1)} copy-done((bf16[1,360,2880]{2,1,0:T(8,128)(2,1)S(1)}, bf16[1,360,2880]{2,1,0:T(8,128)(2,1)}, u32[]{:S(2)}) %copy-start.4) | copy-done | bytes 2073624
  60.0 1.3 %copy.17 = bf16[1,360,2880]{2,1,0:T(8,128)(2,1)} copy(bf16[1,360,2880]{2,1,0:T(8,128)(2,1)S(1)} %copy-done.4) | data formatting | bytes 4147200
  61.3 0.7 %copy.18 = bf16[1,64,2880]{2,1,0:T(8,128)(2,1)} copy(bf16[1,64,2880]{2,1,0:T(8,128)(2,1)S(1)} %get-tuple-element.11) | data formatting | bytes 737280
Async XLA Ops:
  0.6 1.0 %copy-start = (bf16[1,64,2880]{2,1,0:T(8,128)(2,1)S(1)}, bf16[1,64,2880]{2,1,0:T(8,128)(2,1)}, u32[]{:S(2)}) copy-start(bf16[1,64,2880]{2,1,0:T(8,128)(2,1)} %x_hbm.1) | copy-start | bytes 1105924
  1.6 1.0 %copy-start.1 = (bf16[1,64,2880]{2,1,0:T(8,128)(2,1)S(1)}, bf16[1,64,2880]{2,1,0:T(8,128)(2,1)}, u32[]{:S(2)}) copy-start(bf16[1,64,2880]{2,1,0:T(8,128)(2,1)} %g_hbm.1) | copy-start | bytes 1105924
  2.6 0.7 %copy-start.2 = (s32[1,64,4]{1,2,0:T(4,128)S(1)}, s32[1,64,4]{1,2,0:T(4,128)}, u32[]{:S(2)}) copy-start(s32[1,64,4]{1,2,0:T(4,128)} %param.9) | copy-start | bytes 3076
  3.3 0.7 %copy-start.3 = (f32[1,64,4]{1,2,0:T(4,128)S(1)}, f32[1,64,4]{1,2,0:T(4,128)}, u32[]{:S(2)}) copy-start(f32[1,64,4]{1,2,0:T(4,128)} %param.10) | copy-start | bytes 3076
  57.6 2.4 %copy-start.4 = (bf16[1,360,2880]{2,1,0:T(8,128)(2,1)S(1)}, bf16[1,360,2880]{2,1,0:T(8,128)(2,1)}, u32[]{:S(2)}) copy-start(bf16[1,360,2880]{2,1,0:T(8,128)(2,1)} %get-tuple-element.10) | copy-start | bytes 6220804

commit v2 on v1

v2 whole, which is shorter than its diff:
```python
import jax
import jax.numpy as jnp
from jax import lax
from jax.experimental import pallas as pl
from jax.experimental.pallas import tpu as pltpu
from jax.sharding import PartitionSpec as P

D = 2880
HS = 360
TOK = 64
FLIGHT = 4
NX = 4
NZ = 8
HALF = 1408
WIDE = D - HALF
CHUNKS = ((0, 512), (512, 1024), (1024, WIDE))
ORDER = (0, 4, 1, 5, 2, 6, 3, 7)
LAG = 3
NCH = len(CHUNKS)
MESH = pl.DeviceIdType.MESH
F32 = jnp.float32
BF16 = jnp.bfloat16


def nt(left, right):
    return lax.dot_general(left, right, (((1,), (1,)), ((), ())), preferred_element_type=F32)


def nn(left, right):
    return jnp.dot(left, right, preferred_element_type=F32)


def selector(ids, rows, per_expert):
    row = lax.broadcasted_iota(jnp.int32, (rows, TOK), 0)
    owner = row // per_expert
    matches = [ids[k : k + 1, :] == owner for k in range(4)]
    hit = matches[0] | matches[1] | matches[2] | matches[3]
    before = lax.broadcasted_iota(jnp.int32, (TOK, TOK), 0)
    token = lax.broadcasted_iota(jnp.int32, (TOK, TOK), 1)
    earlier = jnp.where(before < token, 1.0, 0.0).astype(BF16)
    rank = nn(jnp.where(hit, 1.0, 0.0).astype(BF16), earlier)
    return jnp.where(hit & (rank == (row % 4).astype(F32)), 1.0, 0.0), matches, row % 8 < 4


def kernel(x_hbm, g_hbm, ids_hbm, pr_hbm, wg_hbm, wu_hbm, wd_hbm, *refs):
    gg_o, gu_o, gd_o, sel_o = refs[:4]
    f_o = refs[4 : 4 + NCH]
    refs = refs[4 + NCH :]
    q1s, ts, hs = (refs[j * NCH : (j + 1) * NCH] for j in range(3))
    (
        x_v, g_v, ids_v, ids2_v, pr_v, wg_v, wu_v, wd_v, send_v, rows_v, part_v,
        lsem, sem_z, sem_p, sem_x, sem_f, sem_r, sem_ids, s1, r1, s2, r2,
    ) = refs[3 * NCH :]
    pipe = lax.axis_index("pipe")
    me = lax.axis_index("expert")
    z = lax.div(me, NX)
    x = lax.rem(me, NX)
    xr = lax.rem(x + 1, NX)
    xl = lax.rem(x + NX - 1, NX)
    xo = lax.rem(x + 2, NX)

    def same(zz, xx):
        return {"pipe": pipe, "expert": zz * NX + xx}

    loads = [
        pltpu.make_async_copy(src.at[0], dst, lsem.at[i])
        for i, (src, dst) in enumerate(
            (
                (ids_hbm, ids_v),
                (pr_hbm, pr_v),
                (x_hbm, x_v),
                (g_hbm, g_v),
                (wg_hbm, wg_v),
                (wu_hbm, wu_v),
                (wd_hbm, wd_v),
            )
        )
    ]
    for load in loads:
        load.start()

    barrier = pltpu.get_barrier_semaphore()
    for d in range(1, NZ):
        pl.semaphore_signal(barrier, 1, device_id=same(lax.rem(z + d, NZ), x), device_id_type=MESH)
    t = 2 * lax.rem(z, 2) - 1
    pair = z - t
    for xn in (xl, xr, xo):
        pl.semaphore_signal(barrier, 1, device_id=same(z, xn), device_id_type=MESH)
        pl.semaphore_signal(barrier, 1, device_id=same(pair, xn), device_id_type=MESH)

    def column(shift, steps):
        zz = lax.rem(z + t * steps + NZ, NZ)
        return {"pipe": pipe + shift, "expert": zz * NX + x}

    @pl.when(pipe > 0)
    def _():
        for steps in (0, 1, 2, 3):
            pl.semaphore_signal(barrier, 1, device_id=column(-1, steps), device_id_type=MESH)

    @pl.when(pipe < 7)
    def _():
        for steps in (0, 1, -2, 3):
            pl.semaphore_signal(barrier, 1, device_id=column(1, steps), device_id_type=MESH)

    loads[0].wait()
    loads[1].wait()
    ids = ids_v[...]
    sel, matches, is_in = selector(ids, 32, 8)
    probs = pr_v[...]
    weight = jnp.zeros((32, TOK), F32)
    for k in range(4):
        weight = weight + jnp.where(matches[k], probs[k : k + 1, :], 0.0)
    weight_col = jnp.sum(weight * sel, axis=1, keepdims=True)
    sel_in = jnp.where(is_in, sel, 0.0).astype(BF16)
    sel_co = jnp.where(is_in, 0.0, sel).astype(BF16)
    loads[2].wait()
    loads[3].wait()
    picked = nn(sel_in, x_v[...]) + nn(sel_co, g_v[...]) * weight_col
    send_v[...] = picked.reshape(FLIGHT, 8, D).astype(BF16)

    pl.semaphore_wait(barrier, jnp.where((pipe == 0) | (pipe == 7), 17, 21))

    odd = lax.rem(z, 2)

    def slot(parity, i):
        return (3 - i) + parity * (1 + 2 * i)

    def place(i):
        return slot(odd, i) if i < 4 else slot(1 - odd, i - 4)

    def arrived(xs, i):
        b = (xs, place(i))
        return pltpu.make_async_remote_copy(
            rows_v.at[b], rows_v.at[b], sem_z.at[0], sem_r.at[b],
            device_id=same(z, xr), device_id_type=MESH,
        )

    sends = []

    def send(src, at, to, sem):
        sends.append(
            pltpu.make_async_remote_copy(
                src, rows_v.at[at], sem, sem_r.at[at], device_id=to, device_id_type=MESH
            )
        )
        sends[-1].start()

    def push(i):
        src = send_v.at[lax.div(z, 2)] if i == 0 else rows_v.at[x, place(i)]
        if i < 4:
            send(src, (x, place(i)), same(pair, x), sem_p.at[i])
        send(src, (x, place(i)), same(z, xr), sem_x.at[0, i])
        send(src, (x, place(i)), same(z, xl), sem_x.at[1, i])

    def forward(n, i):
        arrived(xl, i).wait_recv()
        arrived(xr, i).wait_recv()
        here, to = (xl, xr) if n % 2 == 0 else (xr, xl)
        send(rows_v.at[here, place(i)], (here, place(i)), same(z, to), sem_f.at[i])

    push(0)
    for j, step in enumerate((t, -2 * t, 3 * t)):
        zt = lax.rem(z + step + NZ, NZ)
        parity = odd if j == 1 else 1 - odd
        send(send_v.at[lax.div(zt, 2)], (x, slot(parity, j + 1)), same(zt, x), sem_z.at[j])
    own = pltpu.make_async_copy(send_v.at[lax.div(z, 2)], rows_v.at[x, place(0)], sem_r.at[x, place(0)])
    own.start()

    @pl.when(pipe > 0)
    def _():
        pltpu.make_async_remote_copy(
            ids_v, ids2_v, sem_ids.at[0], sem_ids.at[1],
            device_id={"pipe": pipe - 1, "expert": me}, device_id_type=MESH,
        ).start()

    for n, i in enumerate(ORDER):
        if i > 0:
            arrived(x, i).wait_recv()
            push(i)
        if n >= LAG:
            forward(n - LAG, ORDER[n - LAG])
    for n in range(NZ - LAG, NZ):
        forward(n, ORDER[n])
    own.wait()
    for load in loads[4:]:
        load.wait()
    for i in ORDER:
        arrived(xo, i).wait_recv()

    rows = rows_v[...].reshape(256, D)
    pre_gate = nt(wg_v[...], rows)
    pre_up = nt(wu_v[...], rows)
    hidden_grad = pltpu.roll(nt(wd_v[...], rows), 252, 1)
    in_col = lax.broadcasted_iota(jnp.int32, (HS, 256), 1) % 8 < 4
    sigma = jax.nn.sigmoid(pre_gate)
    silu = pre_gate * sigma
    slope = sigma * (1.0 + pre_gate * (1.0 - sigma))
    hidden = jnp.where(in_col, silu * pre_up, 0.0)
    d_gate = jnp.where(in_col, hidden_grad * pre_up * slope, 0.0)
    d_up = jnp.where(in_col, hidden_grad * silu, 0.0)
    hidden_co = pltpu.roll(hidden, 4, 1).astype(BF16)
    gate_lo = d_gate.T.astype(BF16)
    up_lo = d_up.T.astype(BF16)
    gate_hi = pltpu.roll(d_gate, 4, 1).T.astype(BF16)
    up_hi = pltpu.roll(d_up, 4, 1).T.astype(BF16)
    d_gate = d_gate.astype(BF16)
    d_up = d_up.astype(BF16)

    group = lax.div(z, 2)
    members = [(xn, flip) for xn, flip in ((xo, 1), (xo, 0), (xr, 1), (xl, 1), (xr, 0), (xl, 0), (x, 1))]

    def step1(k, j, xn, flip):
        c0, c1 = CHUNKS[k]
        half = odd + flip - 2 * odd * flip
        return pltpu.make_async_remote_copy(
            part_v.at[xn, half, :, pl.ds(c0, c1 - c0)], q1s[k].at[x, odd], s1.at[k, j], r1.at[k, x, odd],
            device_id=same(pair if flip else z, xn), device_id_type=MESH,
        )

    def step2(k, r):
        zt = lax.rem(2 * group - 3 + 4 * odd + r + NZ, NZ)
        return pltpu.make_async_remote_copy(
            ts[k].at[r], hs[k].at[group], s2.at[k, r], r2.at[k, group],
            device_id={"pipe": pipe - 1, "expert": zt * NX + x}, device_id_type=MESH,
        )

    def partials(k):
        c0, c1 = CHUNKS[k]
        lo1 = min(c1, HALF)
        low = nn(gate_lo, wg_v[:, c0:lo1]) + nn(up_lo, wu_v[:, c0:lo1])
        high = nn(gate_hi, wg_v[:, HALF + c0 : HALF + c1]) + nn(up_hi, wu_v[:, HALF + c0 : HALF + c1])
        part_v[:, :, :, c0:lo1] = (low + high[:, : lo1 - c0]).astype(BF16).reshape(NX, 2, 32, lo1 - c0)
        if c1 > lo1:
            part_v[:, :, :, lo1:c1] = high[:, lo1 - c0 :].astype(BF16).reshape(NX, 2, 32, c1 - lo1)
        for j, (xn, flip) in enumerate(members):
            step1(k, j, xn, flip).start()

    def across(k):
        c0, c1 = CHUNKS[k]
        total = part_v[x, odd, :, c0:c1].astype(F32)
        for xn, flip in reversed(members):
            half = odd + flip - 2 * odd * flip
            pltpu.make_async_remote_copy(
                part_v.at[x, odd, :, pl.ds(c0, c1 - c0)], q1s[k].at[xn, half], s1.at[k, 0], r1.at[k, xn, half],
                device_id=same(pair, xn), device_id_type=MESH,
            ).wait_recv()
            total = total + q1s[k][xn, half].astype(F32)
        ts[k][...] = total.reshape(4, 8, c1 - c0).astype(BF16)

        @pl.when(pipe > 0)
        def _():
            for r in range(4):
                step2(k, r).start()

    def grads(left, out):
        out[0] = nn(left, rows_v[...].reshape(256, D)).astype(BF16)

    for k in range(NCH):
        partials(k)
    grads(hidden_co, gd_o)

    @pl.when(pipe == 7)
    def _():
        sel_o[...] = jnp.zeros_like(sel_o)
        for k in range(NCH):
            f_o[k][...] = jnp.zeros_like(f_o[k])

    @pl.when(pipe < 7)
    def _():
        pltpu.make_async_remote_copy(
            ids_v, ids2_v, sem_ids.at[0], sem_ids.at[1],
            device_id={"pipe": pipe, "expert": me}, device_id_type=MESH,
        ).wait_recv()
        sel2, _, low_half = selector(ids2_v[...], 32, 8)
        sel_o[0] = jnp.where(low_half, sel2, 0.0).T.astype(BF16)
        sel_o[1] = jnp.where(low_half, 0.0, sel2).T.astype(BF16)

    grads(d_gate, gg_o)
    across(0)
    grads(d_up, gu_o)
    for k in range(1, NCH):
        across(k)

    @pl.when(pipe < 7)
    def _():
        for k in range(NCH):
            for e in range(FLIGHT):
                pltpu.make_async_remote_copy(
                    ts[k].at[0], hs[k].at[e], s2.at[k, 0], r2.at[k, e],
                    device_id={"pipe": pipe, "expert": me}, device_id_type=MESH,
                ).wait_recv()
            f_o[k][...] = hs[k][...].reshape(f_o[k].shape)

    for copy in sends:
        copy.wait_send()
    for k in range(NCH):
        for j, (xn, flip) in enumerate(members):
            step1(k, j, xn, flip).wait_send()

    @pl.when(pipe > 0)
    def _():
        pltpu.make_async_remote_copy(
            ids_v, ids2_v, sem_ids.at[0], sem_ids.at[1],
            device_id={"pipe": pipe - 1, "expert": me}, device_id_type=MESH,
        ).wait_send()
        for k in range(NCH):
            for r in range(4):
                step2(k, r).wait_send()


def finish(gg_i, gu_i, gd_i, sel_i, *refs):
    f_i = refs[:NCH]
    gg_hbm, gu_hbm, gd_hbm, gp_hbm, gp_v, sem = refs[NCH:]
    copies = [
        pltpu.make_async_copy(src, dst, sem.at[i])
        for i, (src, dst) in enumerate(((gg_i, gg_hbm), (gu_i, gu_hbm), (gd_i, gd_hbm), (gp_v, gp_hbm)))
    ]
    for copy in copies[:3]:
        copy.start()
    for k, (c0, c1) in enumerate(CHUNKS):
        lo1 = min(c1, HALF)
        got = f_i[k][...]
        gp_v[0, :, c0:lo1] = nn(sel_i[0], got[:, : lo1 - c0]).astype(BF16)
        gp_v[0, :, HALF + c0 : HALF + c1] = nn(sel_i[1], got).astype(BF16)
    copies[3].start()
    for copy in copies:
        copy.wait()


def hbm(value):
    return pltpu.with_memory_space_constraint(value, pltpu.HBM)


def body(layer_input, grad_output, expert_ids, gate_probs, w_gate, w_up, w_down):
    ids = jnp.transpose(expert_ids, (0, 2, 1))
    probs = jnp.transpose(gate_probs, (0, 2, 1))
    dma = pltpu.SemaphoreType.DMA
    widths = [c1 - c0 for c0, c1 in CHUNKS]
    wide = (HS, D)
    vmem = pl.BlockSpec(memory_space=pltpu.VMEM)
    anywhere = pl.BlockSpec(memory_space=pl.ANY)
    made = pl.pallas_call(
        kernel,
        out_shape=[pltpu.VMEM((1, HS, D), BF16)] * 3
        + [pltpu.VMEM((2, 64, 32), BF16)]
        + [pltpu.VMEM((32, w), BF16) for w in widths],
        in_specs=[anywhere] * 7,
        out_specs=[vmem] * (4 + NCH),
        scratch_shapes=[pltpu.VMEM((NX, 2, 32, w), BF16) for w in widths]
        + [pltpu.VMEM((FLIGHT, 8, w), BF16) for w in widths] * 2
        + [
            pltpu.VMEM((TOK, D), BF16),
            pltpu.VMEM((TOK, D), BF16),
            pltpu.VMEM((4, TOK), jnp.int32),
            pltpu.VMEM((4, TOK), jnp.int32),
            pltpu.VMEM((4, TOK), F32),
            pltpu.VMEM(wide, BF16),
            pltpu.VMEM(wide, BF16),
            pltpu.VMEM(wide, BF16),
            pltpu.VMEM((FLIGHT, 8, D), BF16),
            pltpu.VMEM((NX, NZ, 8, D), BF16),
            pltpu.VMEM((NX, 2, 32, WIDE), BF16),
            dma((7,)),
            dma((3,)),
            dma((4,)),
            dma((2, NZ)),
            dma((NZ,)),
            dma((NX, NZ)),
            dma((2,)),
            dma((NCH, 7)),
            dma((NCH, NX, 2)),
            dma((NCH, 4)),
            dma((NCH, FLIGHT)),
        ],
        compiler_params=pltpu.CompilerParams(
            collective_id=0, has_side_effects=True, vmem_limit_bytes=40 * 1024 * 1024
        ),
    )(*map(hbm, (layer_input, grad_output, ids, probs, w_gate, w_up, w_down)))
    return tuple(
        pl.pallas_call(
            finish,
            out_shape=[jax.ShapeDtypeStruct((1, HS, D), BF16)] * 3 + [jax.ShapeDtypeStruct((1, TOK, D), BF16)],
            in_specs=[vmem] * (4 + NCH),
            out_specs=[anywhere] * 4,
            scratch_shapes=[pltpu.VMEM((1, TOK, D), BF16), dma((4,))],
            compiler_params=pltpu.CompilerParams(vmem_limit_bytes=16 * 1024 * 1024),
        )(*made)
    )


def solution(mesh):
    spec = P("pipe", "expert", None)
    return jax.shard_map(body, mesh=mesh, in_specs=(spec,) * 7, out_specs=(spec,) * 4, check_vma=False)
```

time: 62.3 us -> 52.5 us (0.84)
  local copies, waits for them, and re-layouts: 9.09 us -> 0 us
    unnamed x14 -> x0, local copies, waits for them, and re-layouts: 9.09 us -> none
    pallas_call x1 -> x2, Pallas kernels: 52.3 us -> 51.8 us  [the longest x1 49 us: body(): pl.pallas_call(kernel, out_shape=[pltpu.VMEM((1, HS, D), BF16)] * 3 + [pl...]
where the time goes in v2:
time: 52.5 us; the launch traced here: 52.4 us
  Pallas kernels  51.8 us (99%)
  between operations  0.64 us (1%)
    pallas_call x1, Pallas kernels, body(): pl.pallas_call(kernel, out_shape=[pltpu.VMEM((1, HS, D), BF16)] * 3 + [pl...  49 us
    pallas_call x1, Pallas kernels, body(): pl.pallas_call(finish, out_shape=[jax.ShapeDtypeStruct((1, HS, D), BF16)]...  2.81 us

profile of v2, /device:TPU:1, one launch (start us, length us, event | category | flops | bytes accessed | tf_op | source)
XLA Modules:
  0.0 52.4 jit_solution(213896929376873814)
XLA Ops:
  0.6 49.0 %shard_map.102 = (bf16[1,360,2880]{2,1,0:T(8,128)(2,1)S(1)}, bf16[1,360,2880]{2,1,0:T(8,128)(2,1)S(1)}, bf16[1,360,2880]{2,1,0:T(8,128)(2,1)S(1)}, bf16[2,64,32]...) custom-call(bf16[1,64,2880]{2,1,0:T(8,128)(2,1)} %x_hbm.1, ...), custom_call_target="tpu_custom_call" | custom-call | tf_op jit(solution)/shard_map/pallas_call | solution.py:342
  49.6 2.8 %shard_map.103 = (bf16[1,360,2880]{2,1,0:T(8,128)(2,1)}, bf16[1,360,2880]{2,1,0:T(8,128)(2,1)}, bf16[1,360,2880]{2,1,0:T(8,128)(2,1)}, bf16[1,64,2880]{2,1,0:T(8,128)(2,1)}) custom-call(bf16[1,360,2880]{2,1,0:T(8,128)(2,1)S(1)} %get-tuple-element.11.gg_i, bf16[1,360,2880]{2,1,0:T(8,128)(2,1)S(1)} %get-tuple-element.12.gu_i, ...), custom_call_target="tpu_custom_call" | custom-call | tf_op jit(solution)/shard_map/pallas_call | solution.py:380

commit v3 on v2

--- a/solution.py
+++ b/solution.py
@@ -16,6 +16,7 @@
 CHUNKS = ((0, 512), (512, 1024), (1024, WIDE))
 ORDER = (0, 4, 1, 5, 2, 6, 3, 7)
 LAG = 3
+GATE = 0
 NCH = len(CHUNKS)
 MESH = pl.DeviceIdType.MESH
 F32 = jnp.float32
@@ -49,7 +50,7 @@
     q1s, ts, hs = (refs[j * NCH : (j + 1) * NCH] for j in range(3))
     (
         x_v, g_v, ids_v, ids2_v, pr_v, wg_v, wu_v, wd_v, send_v, rows_v, part_v,
-        lsem, sem_z, sem_p, sem_x, sem_f, sem_r, sem_ids, s1, r1, s2, r2,
+        lsem, sem_z, sem_p, sem_x, sem_f, sem_r, sem_ids, s1, r1, s2, r2, gate,
     ) = refs[3 * NCH :]
     pipe = lax.axis_index("pipe")
     me = lax.axis_index("expert")
@@ -158,6 +159,10 @@
         here, to = (xl, xr) if n % 2 == 0 else (xr, xl)
         send(rows_v.at[here, place(i)], (here, place(i)), same(z, to), sem_f.at[i])
 
+    @pl.when(lax.rem(pipe, 2) == 1)
+    def _():
+        pl.semaphore_wait(gate, 1)
+
     push(0)
     for j, step in enumerate((t, -2 * t, 3 * t)):
         zt = lax.rem(z + step + NZ, NZ)
@@ -177,6 +182,14 @@
         if i > 0:
             arrived(x, i).wait_recv()
             push(i)
+        if n == GATE:
+
+            @pl.when(lax.rem(pipe, 2) == 0)
+            def _():
+                pl.semaphore_signal(
+                    gate, 1, device_id={"pipe": pipe + 1, "expert": me}, device_id_type=MESH
+                )
+
         if n >= LAG:
             forward(n - LAG, ORDER[n - LAG])
     for n in range(NZ - LAG, NZ):
@@ -275,10 +288,11 @@
         sel_o[0] = jnp.where(low_half, sel2, 0.0).T.astype(BF16)
         sel_o[1] = jnp.where(low_half, 0.0, sel2).T.astype(BF16)
 
+    across(0)
     grads(d_gate, gg_o)
-    across(0)
+    across(1)
     grads(d_up, gu_o)
-    for k in range(1, NCH):
+    for k in range(2, NCH):
         across(k)
 
     @pl.when(pipe < 7)
@@ -371,6 +385,7 @@
             dma((NCH, NX, 2)),
             dma((NCH, 4)),
             dma((NCH, FLIGHT)),
+            pltpu.SemaphoreType.REGULAR,
         ],
         compiler_params=pltpu.CompilerParams(
             collective_id=0, has_side_effects=True, vmem_limit_bytes=40 * 1024 * 1024

time: 52.5 us -> 52.2 us (level)
  no operation moved by 1% of the time
where the time goes in v3:
time: 52.2 us; the launch traced here: 52.1 us
  Pallas kernels  51.5 us (99%)
  between operations  0.64 us (1%)
    pallas_call x1, Pallas kernels, body(): pl.pallas_call(kernel, out_shape=[pltpu.VMEM((1, HS, D), BF16)] * 3 + [pl...  48.7 us
    pallas_call x1, Pallas kernels, body(): pl.pallas_call(finish, out_shape=[jax.ShapeDtypeStruct((1, HS, D), BF16)]...  2.81 us

profile of v3, /device:TPU:1, one launch (start us, length us, event | category | flops | bytes accessed | tf_op | source)
XLA Modules:
  0.0 52.1 jit_solution(14404459238738511257)
XLA Ops:
  0.6 48.7 %shard_map.102 = (bf16[1,360,2880]{2,1,0:T(8,128)(2,1)S(1)}, bf16[1,360,2880]{2,1,0:T(8,128)(2,1)S(1)}, bf16[1,360,2880]{2,1,0:T(8,128)(2,1)S(1)}, bf16[2,64,32]...) custom-call(bf16[1,64,2880]{2,1,0:T(8,128)(2,1)} %x_hbm.1, ...), custom_call_target="tpu_custom_call" | custom-call | tf_op jit(solution)/shard_map/pallas_call | solution.py:356
  49.3 2.8 %shard_map.103 = (bf16[1,360,2880]{2,1,0:T(8,128)(2,1)}, bf16[1,360,2880]{2,1,0:T(8,128)(2,1)}, bf16[1,360,2880]{2,1,0:T(8,128)(2,1)}, bf16[1,64,2880]{2,1,0:T(8,128)(2,1)}) custom-call(bf16[1,360,2880]{2,1,0:T(8,128)(2,1)S(1)} %get-tuple-element.11.gg_i, bf16[1,360,2880]{2,1,0:T(8,128)(2,1)S(1)} %get-tuple-element.12.gu_i, ...), custom_call_target="tpu_custom_call" | custom-call | tf_op jit(solution)/shard_map/pallas_call | solution.py:395

commit v4 on v3

--- a/solution.py
+++ b/solution.py
@@ -14,7 +14,7 @@
 HALF = 1408
 WIDE = D - HALF
 CHUNKS = ((0, 512), (512, 1024), (1024, WIDE))
-ORDER = (0, 4, 1, 5, 2, 6, 3, 7)
+ORDER = (0, 1, 4, 2, 5, 3, 6, 7)
 LAG = 3
 GATE = 0
 NCH = len(CHUNKS)
@@ -148,10 +148,10 @@
 
     def push(i):
         src = send_v.at[lax.div(z, 2)] if i == 0 else rows_v.at[x, place(i)]
+        send(src, (x, place(i)), same(z, xr), sem_x.at[0, i])
+        send(src, (x, place(i)), same(z, xl), sem_x.at[1, i])
         if i < 4:
             send(src, (x, place(i)), same(pair, x), sem_p.at[i])
-        send(src, (x, place(i)), same(z, xr), sem_x.at[0, i])
-        send(src, (x, place(i)), same(z, xl), sem_x.at[1, i])
 
     def forward(n, i):
         arrived(xl, i).wait_recv()

time: 52.2 us -> 52.7 us (level)
  no operation moved by 1% of the time
where the time goes in v4:
time: 52.7 us; the launch traced here: 52.6 us
  Pallas kernels  52 us (99%)
  between operations  0.64 us (1%)
    pallas_call x1, Pallas kernels, body(): pl.pallas_call(kernel, out_shape=[pltpu.VMEM((1, HS, D), BF16)] * 3 + [pl...  49.2 us
    pallas_call x1, Pallas kernels, body(): pl.pallas_call(finish, out_shape=[jax.ShapeDtypeStruct((1, HS, D), BF16)]...  2.81 us

profile of v4, /device:TPU:1, one launch (start us, length us, event | category | flops | bytes accessed | tf_op | source)
XLA Modules:
  0.0 52.6 jit_solution(3257641625497439644)
XLA Ops:
  0.6 49.2 %shard_map.102 = (bf16[1,360,2880]{2,1,0:T(8,128)(2,1)S(1)}, bf16[1,360,2880]{2,1,0:T(8,128)(2,1)S(1)}, bf16[1,360,2880]{2,1,0:T(8,128)(2,1)S(1)}, bf16[2,64,32]...) custom-call(bf16[1,64,2880]{2,1,0:T(8,128)(2,1)} %x_hbm.1, ...), custom_call_target="tpu_custom_call" | custom-call | tf_op jit(solution)/shard_map/pallas_call | solution.py:356
  49.8 2.8 %shard_map.103 = (bf16[1,360,2880]{2,1,0:T(8,128)(2,1)}, bf16[1,360,2880]{2,1,0:T(8,128)(2,1)}, bf16[1,360,2880]{2,1,0:T(8,128)(2,1)}, bf16[1,64,2880]{2,1,0:T(8,128)(2,1)}) custom-call(bf16[1,360,2880]{2,1,0:T(8,128)(2,1)S(1)} %get-tuple-element.11.gg_i, bf16[1,360,2880]{2,1,0:T(8,128)(2,1)S(1)} %get-tuple-element.12.gu_i, ...), custom_call_target="tpu_custom_call" | custom-call | tf_op jit(solution)/shard_map/pallas_call | solution.py:395
